TPU v7x, 32 devices: a whole 2x2x4 slice. The times are simulated.
32 devices in a mesh: gx: 8 (over z, core), gy: 4 (over y, x).
Axes of the slice: x: 2, y: 2, z: 4, core: 2. Of those that a mesh axis runs over, the one named last changes fastest.
Arguments:
- suction_potential: float32 [64, 32, 128], P('gx', 'gy'), may hold values from -3 to 0.3
- ground_warmth: float32 [64, 32, 128], P('gx', 'gy'), may hold values from -4 to 4
- ground_category: int32 [64, 32, 128], P('gx', 'gy'), may hold values from 0 to 11
- icebound_flag: int32 [64, 32, 128], P('gx', 'gy'), may hold values 0 or 1
- ground_wetted_permeability: float32 [12], replicated, may hold values from 0.02 to 0.15
- ground_falloff_exponent: float32 [12], replicated, may hold values from 0.3 to 1.5
- camera_skew_per_plane: float32 [4], replicated, may hold values from -1 to 1
- hue_gradient_steepness: float32 [3], replicated, may hold values from 4 to 16
- hue_gradient_middles: float32 [3], replicated, may hold values from 0.1 to 0.4
- camera_distance_ordering: int32 [4, 4], replicated, may hold values from 0 to 3, as said below
Outputs:
- head_out: float32 [64, 32, 128], P('gx', 'gy')
- temp_out: float32 [64, 32, 128], P('gx', 'gy')
- image: float32 [4, 4, 64, 128], P(None, None, 'gx', 'gy')
Inputs may be any that keep to these rules, and one draw needn't show every extreme that they name: Each row of camera_distance_ordering names every slab 0 to 3 once.
All inputs are finite; a program needn't handle non-finite values. No bound on the sum of `icebound_flag` on one device may be relied on, other than what follows from the above.
Results may differ from a plain program's by a relative error of at most 0.0003.
Values sent between devices are 32-bit elements; how exact they have to be, the bound alone decides.
No kernel may reach another device: no remote copies, remote signals or barrier semaphores. Data moves between devices by JAX's collectives and lax.ppermute only.
A program may use at most 64 MiB of HBM per device.

v0:
```python
import jax
import jax.numpy as jnp
from jax import lax
from jax.sharding import PartitionSpec as P

STEPS = 2
IMPEDANCE = 4.0
DIFFUSE = 0.12


def with_halo(x, sides, width):
    for axis, dim in sides:
        count, length = (lax.axis_size(axis), x.shape[dim])
        up = [(i, (i + 1) % count) for i in range(count - 1)]
        down = [(j, i) for i, j in up]
        last = lax.slice_in_dim(x, length - width, length, axis=dim)
        first = lax.slice_in_dim(x, 0, width, axis=dim)
        before = lax.ppermute(last, axis, up)
        after = lax.ppermute(first, axis, down)
        x = jnp.concatenate([before, x, after], axis=dim)
    return x


def voxel_index_map(ground_category, table):
    total = jnp.zeros(ground_category.shape, jnp.float32)
    for number in range(table.shape[0]):
        total = total + jnp.where(ground_category == number, table[number], jnp.float32(0.0))
    return total


def advance(evolving_arrays, first_row, first_col, rows_all, cols_all):
    suction_potential, temp, conduct_sat, alpha, ice = evolving_arrays
    conduct = (
        conduct_sat
        * jnp.exp(alpha * jnp.minimum(suction_potential, 0.0))
        * jnp.exp(-IMPEDANCE * ice * jax.nn.sigmoid(-2.0 * temp))
    )
    global_rows = first_row + jnp.arange(suction_potential.shape[0], dtype=jnp.int32)
    global_cols = first_col + jnp.arange(suction_potential.shape[1], dtype=jnp.int32)
    open_rows = ((global_rows[:-1] >= 0) & (global_rows[1:] <= rows_all - 1))[:, None, None]
    open_cols = ((global_cols[:-1] >= 0) & (global_cols[1:] <= cols_all - 1))[None, :, None]
    flux_rows = jnp.where(
        open_rows,
        0.5 * (conduct[1:] + conduct[:-1]) * (suction_potential[1:] - suction_potential[:-1]),
        0.0,
    )
    flux_cols = jnp.where(
        open_cols,
        0.5
        * (conduct[:, 1:] + conduct[:, :-1])
        * (suction_potential[:, 1:] - suction_potential[:, :-1]),
        0.0,
    )
    flux_up = (
        0.5
        * (conduct[..., 1:] + conduct[..., :-1])
        * (suction_potential[..., 1:] - suction_potential[..., :-1] + 1.0)
    )
    zeros_up = jnp.zeros(suction_potential.shape[:2] + (1,), suction_potential.dtype)
    change_up = jnp.concatenate([flux_up, zeros_up], 2) - jnp.concatenate([zeros_up, flux_up], 2)
    change = (
        flux_rows[1:, 1:-1]
        - flux_rows[:-1, 1:-1]
        + (flux_cols[1:-1, 1:] - flux_cols[1:-1, :-1])
        + change_up[1:-1, 1:-1]
    )
    inside = ((global_rows[1:-1] >= 0) & (global_rows[1:-1] <= rows_all - 1))[:, None, None] & (
        (global_cols[1:-1] >= 0) & (global_cols[1:-1] <= cols_all - 1)
    )[None, :, None]
    head_new = jnp.where(inside, suction_potential[1:-1, 1:-1] + change, 0.0)
    vertical = jnp.concatenate([temp[..., 1:], zeros_up], 2) + jnp.concatenate(
        [zeros_up, temp[..., :-1]], 2
    )
    laplace = (
        temp[2:, 1:-1]
        + temp[:-2, 1:-1]
        + temp[1:-1, 2:]
        + temp[1:-1, :-2]
        + vertical[1:-1, 1:-1]
        - 6.0 * temp[1:-1, 1:-1]
    )
    temp_new = jnp.where(inside, temp[1:-1, 1:-1] + DIFFUSE * laplace, 0.0)
    return (head_new, temp_new, conduct_sat[1:-1, 1:-1], alpha[1:-1, 1:-1], ice[1:-1, 1:-1])


def moisture(suction_potential):
    return 0.05 + 0.4 * jnp.exp(0.8 * jnp.minimum(suction_potential, 0.0))


def render(theta, first_plane, planes_all, groups, tilt, gain, middle):
    depth_z = theta.shape[2]
    planes = first_plane + jnp.arange(theta.shape[1], dtype=jnp.int32)
    shift = tilt * (planes.astype(jnp.float32) - 0.5 * planes_all)
    wrapped = shift - depth_z * jnp.floor(shift / depth_z)
    base = jnp.floor(wrapped)
    frac = wrapped - base
    offset = base.astype(jnp.int32) % depth_z
    doubled = jnp.concatenate([theta, theta], 2)

    def plane_slices(column, start):
        lower_part = lax.dynamic_slice_in_dim(column, start, depth_z, 1)
        upper_part = lax.dynamic_slice_in_dim(column, start + 1, depth_z, 1)
        return (lower_part, upper_part)

    lower_vals, upper_vals = jax.vmap(plane_slices, in_axes=(1, 0), out_axes=(1, 1))(
        doubled, offset
    )
    sample = (1.0 - frac)[None, :, None] * lower_vals + frac[None, :, None] * upper_vals
    shape_four = (theta.shape[0], groups, theta.shape[1] // groups, depth_z)
    sample = sample.reshape(shape_four)
    optical = sample * (8.0 / planes_all)
    before = jnp.cumsum(optical, axis=2) - optical
    weight = (1.0 - jnp.exp(-optical)) * jnp.exp(-before)
    layers = [
        jnp.sum(jax.nn.sigmoid(gain[color] * (sample - middle[color])) * weight, axis=2)
        for color in range(3)
    ]
    layers.append(jnp.sum(optical, axis=2))
    return jnp.stack(layers, 0).transpose(2, 0, 1, 3)


def shards(
    suction_potential,
    ground_warmth,
    ground_category,
    icebound_flag,
    ground_wetted_permeability,
    ground_falloff_exponent,
    camera_skew_per_plane,
    hue_gradient_steepness,
    hue_gradient_middles,
    camera_distance_ordering,
):
    rows_dev = suction_potential.shape[0]
    cols_dev = suction_potential.shape[1]
    rows_all = rows_dev * lax.axis_size("gx")
    cols_all = cols_dev * lax.axis_size("gy")
    row_start = lax.axis_index("gx") * rows_dev
    col_start = lax.axis_index("gy") * cols_dev
    evolving_arrays = (
        suction_potential,
        ground_warmth,
        voxel_index_map(ground_category, ground_wetted_permeability),
        voxel_index_map(ground_category, ground_falloff_exponent),
        icebound_flag.astype(jnp.float32),
    )
    extended = with_halo(jnp.stack(evolving_arrays), (("gx", 1), ("gy", 2)), STEPS)
    evolving_arrays = tuple((extended[number] for number in range(5)))
    for number in range(STEPS):
        margin = STEPS - number
        evolving_arrays = advance(
            evolving_arrays, row_start - margin, col_start - margin, rows_all, cols_all
        )
    theta = moisture(evolving_arrays[0])

    def one_view(tilt):
        return render(
            theta, col_start, cols_all, 1, tilt, hue_gradient_steepness, hue_gradient_middles
        )[0]

    pieces = lax.map(one_view, camera_skew_per_plane)
    received = lax.all_to_all(pieces[None], "gy", split_axis=4, concat_axis=0, tiled=True)
    in_front = (camera_distance_ordering[:, None, :] < camera_distance_ordering[:, :, None]).astype(
        jnp.float32
    )
    depth = received[:, :, 3]
    front = jnp.einsum("vij,jvxz->ivxz", in_front, depth, precision=lax.Precision.HIGHEST)
    color = jnp.sum(jnp.exp(-front)[:, :, None] * received[:, :, :3], axis=0)
    opacity = 1.0 - jnp.exp(-jnp.sum(depth, axis=0))
    image = jnp.concatenate([color, opacity[:, None]], 1)
    return (evolving_arrays[0], evolving_arrays[1], image)


def solution(mesh):
    placed = (
        P("gx", "gy", None),
        P("gx", "gy", None),
        P("gx", "gy", None),
        P("gx", "gy", None),
        P(),
        P(),
        P(),
        P(),
        P(),
        P(),
    )
    return jax.shard_map(
        shards,
        mesh=mesh,
        in_specs=placed,
        out_specs=(P("gx", "gy", None), P("gx", "gy", None), P(None, None, "gx", "gy")),
        check_vma=False,
    )
```

profile of v0, /device:TPU:0, one launch (start us, length us, event | category | flops | bytes accessed | tf_op | source)
XLA Modules:
  0.0 95.9 jit_solution(1274984922315434157)
XLA Ops:
  0.6 1.8 %fusion.79 = (f32[1]{0:T(128)}, f32[1]{0:T(128)}, f32[1]{0:T(128)}, f32[1]{0:T(128)}, f32[1]{0:T(128)}, /*index=5*/f32[1]{0:T(128)}, f32[1]{0:T(128)}, f32[1]{0:...) fusion(f32[12]{0:T(128)} %param.16), kind=kLoop, calls=%fused_computation.171 | loop fusion | bytes 96 | tf_op jit(solution)/shard_map/slice | solution.py:27
  2.4 0.8 bitcast_dynamic-update-slice_fusion.4
  3.2 0.7 fusion.78
  3.9 0.7 copy-done.5
  4.7 7.6 %bitcast_dynamic-update-slice_fusion.2 = (f32[5,8,8,128]{3,2,1,0:T(8,128)S(1)}, pred[8,8,128]{2,1,0:T(8,128)(4,1)S(1)}, pred[8,8,128]{2,1,0:T(8,128)(4,1)S(1)}, ...) fusion(f32[5,8,8,128]{3,2,1,0:T(8,128)S(1)} %bitcast_dynamic-up, ...), kind=kLoop, calls=%fused_computation.130 | loop fusion | flops 286720 | bytes 163888
  12.3 7.6 %bitcast_dynamic-update-slice_fusion.1 = f32[5,8,8,128]{3,2,1,0:T(8,128)S(1)} fusion(f32[5,8,8,128]{3,2,1,0:T(8,128)S(1)} %get-tuple-element.160, pred[8,8,128]{2,1,0:T(8,128)(4,1)S(1)} %get-tuple-element.172, pred[8,8,128]{2,1,0:T(8,128)(4,1)S(1)} %get-tuple-element.171, pred[8,8,128]{2,1,0:T(8,128)(4,1)S(1)} %get-tuple-element.170, ...), kind=kLoop, calls=%fused_computation.129 | loop fusion | flops 188416 | bytes 131120
  19.9 2.4 %collective-permute-start = (f32[5,2,8,128]{3,2,1,0:T(8,128)S(1)}, f32[5,2,8,128]{3,2,1,0:T(8,128)S(1)}, u32[]{:S(2)}, u32[]{:S(2)}) collective-permute-start(f32[5,2,8,128]{3,2,1,0:T(8,128)S(1)} %get-tuple-element.191), channel_id=1, source_target_pairs={{0,4},{4,8},{8,12},{12,16},{16,20},{20,24},{24,28},{1,5},{5,9},{9,... | collective-permute-start | bytes 122888 | tf_op jit(solution)/shard_map/ppermute | solution.py:18
  22.3 1.3 %collective-permute-start.1 = (f32[5,2,8,128]{3,2,1,0:T(8,128)S(1)}, f32[5,2,8,128]{3,2,1,0:T(8,128)S(1)}, u32[]{:S(2)}, u32[]{:S(2)}) collective-permute-start(f32[5,2,8,128]{3,2,1,0:T(8,128)S(1)} %get-tuple-element.192), channel_id=1, source_target_pairs={{4,0},{8,4},{12,8},{16,12},{20,16},{24,20},{28,24},{5,1},{9,5},{13... | collective-permute-start | bytes 122888 | tf_op jit(solution)/shard_map/ppermute | solution.py:19
  24.2 3.4 %collective-permute-done.1 = f32[5,2,8,128]{3,2,1,0:T(8,128)S(1)} collective-permute-done((f32[5,2,8,128]{3,2,1,0:T(8,128)S(1)}, f32[5,2,8,128]{3,2,1,0:T(8,128)S(1)}, u32[]{:S(2)}, u32[]{:S(2)}) %collective-permute-start.1) | collective-permute-done | bytes 40992 | tf_op jit(solution)/shard_map/ppermute | solution.py:19
  27.7 3.4 %collective-permute-start.2 = (f32[5,12,2,128]{3,2,1,0:T(2,128)S(1)}, f32[5,12,2,128]{3,2,1,0:T(2,128)S(1)}, u32[]{:S(2)}, u32[]{:S(2)}) collective-permute-start(f32[5,12,2,128]{3,2,1,0:T(2,128)S(1)} %get-tuple-element.189), channel_id=1, source_target_pairs={{0,1},{1,2},{2,3},{4,5},{5,6},{6,7},{8,9},{9,10},{10,11},{12,13},{... | collective-permute-start | bytes 184328 | tf_op jit(solution)/shard_map/ppermute | solution.py:18
  31.1 1.3 %collective-permute-start.3 = (f32[5,12,2,128]{3,2,1,0:T(2,128)S(1)}, f32[5,12,2,128]{3,2,1,0:T(2,128)S(1)}, u32[]{:S(2)}, u32[]{:S(2)}) collective-permute-start(f32[5,12,2,128]{3,2,1,0:T(2,128)S(1)} %get-tuple-element.190), channel_id=1, source_target_pairs={{1,0},{2,1},{3,2},{5,4},{6,5},{7,6},{9,8},{10,9},{11,10},{13,12},{... | collective-permute-start | bytes 184328 | tf_op jit(solution)/shard_map/ppermute | solution.py:19
  32.9 4.3 %collective-permute-done.3 = f32[5,12,2,128]{3,2,1,0:T(2,128)S(1)} collective-permute-done((f32[5,12,2,128]{3,2,1,0:T(2,128)S(1)}, f32[5,12,2,128]{3,2,1,0:T(2,128)S(1)}, u32[]{:S(2)}, u32[]{:S(2)}) %collective-permute-start.3) | collective-permute-done | bytes 61472 | tf_op jit(solution)/shard_map/ppermute | solution.py:19
  38.3 0.7 multiply_add_fusion.1
  39.8 40.9 %while.12 = (s32[]{:T(128)}, f32[4,4,8,128]{3,2,1,0:T(8,128)S(1)}, f32[3]{0:T(128)S(1)}, f32[4]{0:T(128)S(1)}, s32[]{:T(128)}, /*index=5*/f32[8,8,256]{0,1,2:T(8,128)S(1)}, f32[3]{0:T(128)S(1)}, s32[]{:T(128)}) while((s32[]{:T(128)}, f32[4,4,8,128]{3,2,1,0:T(8,128)S(1)}, f32[3]{0:T(128)S(1)}, f32[4]{0:T(128)S(1)}, s32[]{:T(128)}, ...), condition=%wide.region_6.7_spmd, body=%wide.region_0.6_spmd.sunk | while | flops 352634 | bytes 442941 | solution.py:161
  41.0 1.3 %gather_fusion = f32[8,8,128]{1,0,2:T(8,128)S(1)} fusion(f32[8,8,256]{1,0,2:T(8,128)S(1)} %bitcast.158, s32[8]{0:T(128)S(1)} %get-tuple-element.290), kind=kCustom, calls=%fused_computation.1.clone.1 | custom fusion | bytes 65632 | tf_op jit(solution)/shard_map/while/body/eval_jaxpr/vmap()/gather | solution.py:102
  42.6 1.3 %gather_fusion.1 = f32[8,8,128]{1,0,2:T(8,128)S(1)} fusion(f32[8,8,256]{1,0,2:T(8,128)S(1)} %bitcast.159, s32[8]{0:T(128)S(1)} %get-tuple-element.292), kind=kCustom, calls=%fused_computation.clone.1 | custom fusion | bytes 65632 | tf_op jit(solution)/shard_map/while/body/eval_jaxpr/vmap()/gather | solution.py:101
  44.1 0.7 fusion.83
  45.4 3.9 %fusion.84 = (f32[8,128]{1,0:T(8,128)S(1)}, f32[8,128]{1,0:T(8,128)S(1)}, f32[8,128]{1,0:T(8,128)S(1)}, f32[8,128]{1,0:T(8,128)S(1)}) fusion(f32[]{:T(128)} %bitcast.146, f32[]{:T(128)} %bitcast.147, f32[]{:T(128)} %bitcast.148, f32[]{:T(128)} %bitcast.149, f32[]{:T(128)} %bitcast.150, f32[]{:T(128)} %bitcast.151, f32[8,8,128]{2,1,0:T(8,128)S(1)} %copy.67, ...), kind=kOutput, calls=%fused_computation.16.clone.1 | output fusion | flops 339968 | bytes 82008 | tf_op jit(solution)/shard_map/while/body/eval_jaxpr/jit(cumsum)/reduce_window_sum | solution.py:112
  51.3 1.3 %gather_fusion = f32[8,8,128]{1,0,2:T(8,128)S(1)} fusion(f32[8,8,256]{1,0,2:T(8,128)S(1)} %bitcast.158, s32[8]{0:T(128)S(1)} %get-tuple-element.290), kind=kCustom, calls=%fused_computation.1.clone.1 | custom fusion | bytes 65632 | tf_op jit(solution)/shard_map/while/body/eval_jaxpr/vmap()/gather | solution.py:102
  52.8 1.3 %gather_fusion.1 = f32[8,8,128]{1,0,2:T(8,128)S(1)} fusion(f32[8,8,256]{1,0,2:T(8,128)S(1)} %bitcast.159, s32[8]{0:T(128)S(1)} %get-tuple-element.292), kind=kCustom, calls=%fused_computation.clone.1 | custom fusion | bytes 65632 | tf_op jit(solution)/shard_map/while/body/eval_jaxpr/vmap()/gather | solution.py:101
  54.3 0.7 fusion.83
  55.6 3.9 %fusion.84 = (f32[8,128]{1,0:T(8,128)S(1)}, f32[8,128]{1,0:T(8,128)S(1)}, f32[8,128]{1,0:T(8,128)S(1)}, f32[8,128]{1,0:T(8,128)S(1)}) fusion(f32[]{:T(128)} %bitcast.146, f32[]{:T(128)} %bitcast.147, f32[]{:T(128)} %bitcast.148, f32[]{:T(128)} %bitcast.149, f32[]{:T(128)} %bitcast.150, f32[]{:T(128)} %bitcast.151, f32[8,8,128]{2,1,0:T(8,128)S(1)} %copy.67, ...), kind=kOutput, calls=%fused_computation.16.clone.1 | output fusion | flops 339968 | bytes 82008 | tf_op jit(solution)/shard_map/while/body/eval_jaxpr/jit(cumsum)/reduce_window_sum | solution.py:112
  61.5 1.3 %gather_fusion = f32[8,8,128]{1,0,2:T(8,128)S(1)} fusion(f32[8,8,256]{1,0,2:T(8,128)S(1)} %bitcast.158, s32[8]{0:T(128)S(1)} %get-tuple-element.290), kind=kCustom, calls=%fused_computation.1.clone.1 | custom fusion | bytes 65632 | tf_op jit(solution)/shard_map/while/body/eval_jaxpr/vmap()/gather | solution.py:102
  63.0 1.3 %gather_fusion.1 = f32[8,8,128]{1,0,2:T(8,128)S(1)} fusion(f32[8,8,256]{1,0,2:T(8,128)S(1)} %bitcast.159, s32[8]{0:T(128)S(1)} %get-tuple-element.292), kind=kCustom, calls=%fused_computation.clone.1 | custom fusion | bytes 65632 | tf_op jit(solution)/shard_map/while/body/eval_jaxpr/vmap()/gather | solution.py:101
  65.9 3.9 %fusion.84 = (f32[8,128]{1,0:T(8,128)S(1)}, f32[8,128]{1,0:T(8,128)S(1)}, f32[8,128]{1,0:T(8,128)S(1)}, f32[8,128]{1,0:T(8,128)S(1)}) fusion(f32[]{:T(128)} %bitcast.146, f32[]{:T(128)} %bitcast.147, f32[]{:T(128)} %bitcast.148, f32[]{:T(128)} %bitcast.149, f32[]{:T(128)} %bitcast.150, f32[]{:T(128)} %bitcast.151, f32[8,8,128]{2,1,0:T(8,128)S(1)} %copy.67, ...), kind=kOutput, calls=%fused_computation.16.clone.1 | output fusion | flops 339968 | bytes 82008 | tf_op jit(solution)/shard_map/while/body/eval_jaxpr/jit(cumsum)/reduce_window_sum | solution.py:112
  71.7 1.3 %gather_fusion = f32[8,8,128]{1,0,2:T(8,128)S(1)} fusion(f32[8,8,256]{1,0,2:T(8,128)S(1)} %bitcast.158, s32[8]{0:T(128)S(1)} %get-tuple-element.290), kind=kCustom, calls=%fused_computation.1.clone.1 | custom fusion | bytes 65632 | tf_op jit(solution)/shard_map/while/body/eval_jaxpr/vmap()/gather | solution.py:102
  73.2 1.3 %gather_fusion.1 = f32[8,8,128]{1,0,2:T(8,128)S(1)} fusion(f32[8,8,256]{1,0,2:T(8,128)S(1)} %bitcast.159, s32[8]{0:T(128)S(1)} %get-tuple-element.292), kind=kCustom, calls=%fused_computation.clone.1 | custom fusion | bytes 65632 | tf_op jit(solution)/shard_map/while/body/eval_jaxpr/vmap()/gather | solution.py:101
  76.1 3.9 %fusion.84 = (f32[8,128]{1,0:T(8,128)S(1)}, f32[8,128]{1,0:T(8,128)S(1)}, f32[8,128]{1,0:T(8,128)S(1)}, f32[8,128]{1,0:T(8,128)S(1)}) fusion(f32[]{:T(128)} %bitcast.146, f32[]{:T(128)} %bitcast.147, f32[]{:T(128)} %bitcast.148, f32[]{:T(128)} %bitcast.149, f32[]{:T(128)} %bitcast.150, f32[]{:T(128)} %bitcast.151, f32[8,8,128]{2,1,0:T(8,128)S(1)} %copy.67, ...), kind=kOutput, calls=%fused_computation.16.clone.1 | output fusion | flops 339968 | bytes 82008 | tf_op jit(solution)/shard_map/while/body/eval_jaxpr/jit(cumsum)/reduce_window_sum | solution.py:112
  81.3 1.1 %reshape.252 = f32[4,1,4096]{2,1,0:T(1,128)S(1)} reshape(f32[128,1,4,4,8]{4,3,2,1,0:T(4,128)S(1)} %bitcast_bitcast_fusion) | data formatting | bytes 131072
  82.5 8.5 %all_to_all.18 = f32[4,1,4096]{2,1,0:T(1,128)S(1)} all-to-all(f32[4,1,4096]{2,1,0:T(1,128)S(1)} %reshape.252), channel_id=1, replica_groups=mesh['gx'=8,'gy'=4] {'gy'}, dimensions={0} | all-to-all | bytes 131072 | tf_op jit(solution)/shard_map/all_to_all | solution.py:162
  91.5 0.8 reduce.21
  92.3 1.3 %reshape.253 = f32[128,1,4,4,8]{4,3,2,1,0:T(4,128)S(1)} reshape(f32[4,4096]{1,0:T(4,128)S(1)} %reduce.21) | data formatting | bytes 131072
  (115 shorter events, 19.7 us)
Async XLA Ops:
  2.4 0.8 copy-start.2
  2.4 1.5 %copy-start.3 = (f32[8,8,128]{2,1,0:T(8,128)S(1)}, f32[8,8,128]{2,1,0:T(8,128)}, u32[]{:S(2)}) copy-start(f32[8,8,128]{2,1,0:T(8,128)} %param.13) | copy-start | bytes 98308
  3.9 0.8 copy-start.5
  12.3 7.6 %copy-start.4 = (s32[8,8,128]{2,1,0:T(8,128)S(1)}, s32[8,8,128]{2,1,0:T(8,128)}, u32[]{:S(2)}) copy-start(s32[8,8,128]{2,1,0:T(8,128)} %param.15) | copy-start | bytes 98308
  19.9 4.3 %collective-permute-start = (f32[5,2,8,128]{3,2,1,0:T(8,128)S(1)}, f32[5,2,8,128]{3,2,1,0:T(8,128)S(1)}, u32[]{:S(2)}, u32[]{:S(2)}) collective-permute-start(f32[5,2,8,128]{3,2,1,0:T(8,128)S(1)} %get-tuple-element.191), channel_id=1, source_target_pairs={{0,4},{4,8},{8,12},{12,16},{16,20},{20,24},{24,28},{1,5},{5,9},{9,... | collective-permute-start | bytes 122888 | tf_op jit(solution)/shard_map/ppermute | solution.py:18
  22.3 5.3 %collective-permute-start.1 = (f32[5,2,8,128]{3,2,1,0:T(8,128)S(1)}, f32[5,2,8,128]{3,2,1,0:T(8,128)S(1)}, u32[]{:S(2)}, u32[]{:S(2)}) collective-permute-start(f32[5,2,8,128]{3,2,1,0:T(8,128)S(1)} %get-tuple-element.192), channel_id=1, source_target_pairs={{4,0},{8,4},{12,8},{16,12},{20,16},{24,20},{28,24},{5,1},{9,5},{13... | collective-permute-start | bytes 122888 | tf_op jit(solution)/shard_map/ppermute | solution.py:19
  27.7 5.3 %collective-permute-start.2 = (f32[5,12,2,128]{3,2,1,0:T(2,128)S(1)}, f32[5,12,2,128]{3,2,1,0:T(2,128)S(1)}, u32[]{:S(2)}, u32[]{:S(2)}) collective-permute-start(f32[5,12,2,128]{3,2,1,0:T(2,128)S(1)} %get-tuple-element.189), channel_id=1, source_target_pairs={{0,1},{1,2},{2,3},{4,5},{5,6},{6,7},{8,9},{9,10},{10,11},{12,13},{... | collective-permute-start | bytes 184328 | tf_op jit(solution)/shard_map/ppermute | solution.py:18
  31.1 6.1 %collective-permute-start.3 = (f32[5,12,2,128]{3,2,1,0:T(2,128)S(1)}, f32[5,12,2,128]{3,2,1,0:T(2,128)S(1)}, u32[]{:S(2)}, u32[]{:S(2)}) collective-permute-start(f32[5,12,2,128]{3,2,1,0:T(2,128)S(1)} %get-tuple-element.190), channel_id=1, source_target_pairs={{1,0},{2,1},{3,2},{5,4},{6,5},{7,6},{9,8},{10,9},{11,10},{13,12},{... | collective-permute-start | bytes 184328 | tf_op jit(solution)/shard_map/ppermute | solution.py:19
  39.1 0.7 copy-start
  39.1 0.7 copy-start.1
  39.1 0.7 copy-start.7
  94.2 0.7 copy-start.6
where the time goes:
time: 96.9 us; the launch traced here: 95.9 us
  other arithmetic  39.2 us (40%)
  local copies, waits for them, and re-layouts  30.4 us (31%)
  blocking collectives  8.45 us (9%)
  starting transfers between devices  8.38 us (9%)
  waiting for transfers between devices  8.16 us (8%)
    another operation x4, other arithmetic, render(): before = jnp.cumsum(optical, axis=2) - optical  15.5 us
    unnamed x2, other arithmetic  15.2 us
    all_to_all x1, blocking collectives, shards(): lax.all_to_all(pieces[None], 'gy', split_axis=4, concat_axis=0, tiled=True)  8.45 us
    ppermute x2, waiting for transfers between devices, with_halo(): after = lax.ppermute(first, axis, down)  7.69 us
    gather x8, local copies, waits for them, and re-layouts, plane_slices(): lower_part = lax.dynamic_slice_in_dim(column, start, depth_z, 1)  6.08 us
    gather x8, local copies, waits for them, and re-layouts, plane_slices(): upper_part = lax.dynamic_slice_in_dim(column, start + 1, depth_z, 1)  6 us
    ppermute x2, starting transfers between devices, with_halo(): before = lax.ppermute(last, axis, up)  5.8 us
    unnamed x22, local copies, waits for them, and re-layouts  5.52 us
  transfers between devices with their start and end apart: 4, of which 3 were waited for; matrix products, arithmetic and copies ran while one was open for 1% of the time, Pallas kernels for 0%

commit v1 on v0

--- a/solution.py
+++ b/solution.py
@@ -159,7 +159,10 @@
         )[0]
 
     pieces = lax.map(one_view, camera_skew_per_plane)
-    received = lax.all_to_all(pieces[None], "gy", split_axis=4, concat_axis=0, tiled=True)
+    received = jnp.concatenate(
+        lax.all_to_all(jnp.stack(jnp.split(pieces[None], lax.axis_size("gy"), axis=4)), "gy", 0, 0),
+        axis=0,
+    )
     in_front = (camera_distance_ordering[:, None, :] < camera_distance_ordering[:, :, None]).astype(
         jnp.float32
     )

time: 96.9 us -> 94.1 us (0.971)
  local copies, waits for them, and re-layouts: 30.4 us -> 27.1 us
    unnamed x22 -> x21, local copies, waits for them, and re-layouts: 5.52 us -> 3.34 us
    unnamed x2 -> x3, other arithmetic: 15.2 us -> 15.2 us
where the time goes in v1:
time: 94.1 us; the launch traced here: 93.1 us
  other arithmetic  39.6 us (42%)
  local copies, waits for them, and re-layouts  27.1 us (29%)
  blocking collectives  8.45 us (9%)
  starting transfers between devices  8.38 us (9%)
  waiting for transfers between devices  8.16 us (9%)
    another operation x4, other arithmetic, render(): before = jnp.cumsum(optical, axis=2) - optical  15.7 us
    unnamed x3, other arithmetic  15.2 us
    all_to_all x1, blocking collectives, shards(): lax.all_to_all(jnp.stack(jnp.split(pieces[None], lax.axis_size('gy'), axi...  8.45 us
    ppermute x2, waiting for transfers between devices, with_halo(): after = lax.ppermute(first, axis, down)  7.69 us
    gather x8, local copies, waits for them, and re-layouts, plane_slices(): lower_part = lax.dynamic_slice_in_dim(column, start, depth_z, 1)  6.08 us
    gather x8, local copies, waits for them, and re-layouts, plane_slices(): upper_part = lax.dynamic_slice_in_dim(column, start + 1, depth_z, 1)  6 us
    ppermute x2, starting transfers between devices, with_halo(): before = lax.ppermute(last, axis, up)  5.8 us
    unnamed x21, local copies, waits for them, and re-layouts  3.34 us
  transfers between devices with their start and end apart: 4, of which 3 were waited for; matrix products, arithmetic and copies ran while one was open for 1% of the time, Pallas kernels for 0%

profile of v1, /device:TPU:0, one launch (start us, length us, event | category | flops | bytes accessed | tf_op | source)
XLA Modules:
  0.0 93.1 jit_solution(7099288206636146126)
XLA Ops:
  0.6 1.8 %fusion.79 = (f32[1]{0:T(128)}, f32[1]{0:T(128)}, f32[1]{0:T(128)}, f32[1]{0:T(128)}, f32[1]{0:T(128)}, /*index=5*/f32[1]{0:T(128)}, f32[1]{0:T(128)}, f32[1]{0:...) fusion(f32[12]{0:T(128)} %param.16), kind=kLoop, calls=%fused_computation.177 | loop fusion | bytes 96 | tf_op jit(solution)/shard_map/slice | solution.py:27
  2.4 0.8 bitcast_dynamic-update-slice_fusion.4
  3.2 0.7 fusion.78
  3.9 0.7 copy-done.5
  4.7 7.6 %bitcast_dynamic-update-slice_fusion.2 = (f32[5,8,8,128]{3,2,1,0:T(8,128)S(1)}, pred[8,8,128]{2,1,0:T(8,128)(4,1)S(1)}, pred[8,8,128]{2,1,0:T(8,128)(4,1)S(1)}, ...) fusion(f32[5,8,8,128]{3,2,1,0:T(8,128)S(1)} %bitcast_dynamic-up, ...), kind=kLoop, calls=%fused_computation.136 | loop fusion | flops 286720 | bytes 163888
  12.3 7.5 %bitcast_dynamic-update-slice_fusion.1 = f32[5,8,8,128]{3,2,1,0:T(8,128)S(1)} fusion(f32[5,8,8,128]{3,2,1,0:T(8,128)S(1)} %get-tuple-element.160, pred[8,8,128]{2,1,0:T(8,128)(4,1)S(1)} %get-tuple-element.172, pred[8,8,128]{2,1,0:T(8,128)(4,1)S(1)} %get-tuple-element.171, pred[8,8,128]{2,1,0:T(8,128)(4,1)S(1)} %get-tuple-element.170, ...), kind=kLoop, calls=%fused_computation.135 | loop fusion | flops 188416 | bytes 131120
  19.9 2.4 %collective-permute-start = (f32[5,2,8,128]{3,2,1,0:T(8,128)S(1)}, f32[5,2,8,128]{3,2,1,0:T(8,128)S(1)}, u32[]{:S(2)}, u32[]{:S(2)}) collective-permute-start(f32[5,2,8,128]{3,2,1,0:T(8,128)S(1)} %get-tuple-element.191), channel_id=1, source_target_pairs={{0,4},{4,8},{8,12},{12,16},{16,20},{20,24},{24,28},{1,5},{5,9},{9,... | collective-permute-start | bytes 122888 | tf_op jit(solution)/shard_map/ppermute | solution.py:18
  22.3 1.3 %collective-permute-start.1 = (f32[5,2,8,128]{3,2,1,0:T(8,128)S(1)}, f32[5,2,8,128]{3,2,1,0:T(8,128)S(1)}, u32[]{:S(2)}, u32[]{:S(2)}) collective-permute-start(f32[5,2,8,128]{3,2,1,0:T(8,128)S(1)} %get-tuple-element.192), channel_id=1, source_target_pairs={{4,0},{8,4},{12,8},{16,12},{20,16},{24,20},{28,24},{5,1},{9,5},{13... | collective-permute-start | bytes 122888 | tf_op jit(solution)/shard_map/ppermute | solution.py:19
  24.2 3.4 %collective-permute-done.1 = f32[5,2,8,128]{3,2,1,0:T(8,128)S(1)} collective-permute-done((f32[5,2,8,128]{3,2,1,0:T(8,128)S(1)}, f32[5,2,8,128]{3,2,1,0:T(8,128)S(1)}, u32[]{:S(2)}, u32[]{:S(2)}) %collective-permute-start.1) | collective-permute-done | bytes 40992 | tf_op jit(solution)/shard_map/ppermute | solution.py:19
  27.7 3.4 %collective-permute-start.2 = (f32[5,12,2,128]{3,2,1,0:T(2,128)S(1)}, f32[5,12,2,128]{3,2,1,0:T(2,128)S(1)}, u32[]{:S(2)}, u32[]{:S(2)}) collective-permute-start(f32[5,12,2,128]{3,2,1,0:T(2,128)S(1)} %get-tuple-element.189), channel_id=1, source_target_pairs={{0,1},{1,2},{2,3},{4,5},{5,6},{6,7},{8,9},{9,10},{10,11},{12,13},{... | collective-permute-start | bytes 184328 | tf_op jit(solution)/shard_map/ppermute | solution.py:18
  31.1 1.3 %collective-permute-start.3 = (f32[5,12,2,128]{3,2,1,0:T(2,128)S(1)}, f32[5,12,2,128]{3,2,1,0:T(2,128)S(1)}, u32[]{:S(2)}, u32[]{:S(2)}) collective-permute-start(f32[5,12,2,128]{3,2,1,0:T(2,128)S(1)} %get-tuple-element.190), channel_id=1, source_target_pairs={{1,0},{2,1},{3,2},{5,4},{6,5},{7,6},{9,8},{10,9},{11,10},{13,12},{... | collective-permute-start | bytes 184328 | tf_op jit(solution)/shard_map/ppermute | solution.py:19
  32.9 4.3 %collective-permute-done.3 = f32[5,12,2,128]{3,2,1,0:T(2,128)S(1)} collective-permute-done((f32[5,12,2,128]{3,2,1,0:T(2,128)S(1)}, f32[5,12,2,128]{3,2,1,0:T(2,128)S(1)}, u32[]{:S(2)}, u32[]{:S(2)}) %collective-permute-start.3) | collective-permute-done | bytes 61472 | tf_op jit(solution)/shard_map/ppermute | solution.py:19
  38.3 0.7 multiply_add_fusion.1
  39.8 41.1 %while.12 = (s32[]{:T(128)}, f32[4,4,8,128]{3,2,0,1:T(8,128)S(1)}, f32[3]{0:T(128)S(1)}, f32[4]{0:T(128)S(1)}, s32[]{:T(128)}, /*index=5*/f32[8,8,256]{0,1,2:T(8,128)S(1)}, f32[3]{0:T(128)S(1)}, s32[]{:T(128)}) while((s32[]{:T(128)}, f32[4,4,8,128]{3,2,0,1:T(8,128)S(1)}, f32[3]{0:T(128)S(1)}, f32[4]{0:T(128)S(1)}, s32[]{:T(128)}, ...), condition=%wide.region_6.7_spmd, body=%wide.region_0.6_spmd.sunk | while | flops 352634 | bytes 442941 | solution.py:161
  41.0 1.3 %gather_fusion = f32[8,8,128]{1,0,2:T(8,128)S(1)} fusion(f32[8,8,256]{1,0,2:T(8,128)S(1)} %bitcast.166, s32[8]{0:T(128)S(1)} %get-tuple-element.294), kind=kCustom, calls=%fused_computation.1.clone.1 | custom fusion | bytes 65632 | tf_op jit(solution)/shard_map/while/body/eval_jaxpr/vmap()/gather | solution.py:102
  42.5 1.3 %gather_fusion.1 = f32[8,8,128]{1,0,2:T(8,128)S(1)} fusion(f32[8,8,256]{1,0,2:T(8,128)S(1)} %bitcast.167, s32[8]{0:T(128)S(1)} %get-tuple-element.296), kind=kCustom, calls=%fused_computation.clone.1 | custom fusion | bytes 65632 | tf_op jit(solution)/shard_map/while/body/eval_jaxpr/vmap()/gather | solution.py:101
  44.1 0.7 fusion.84
  45.4 3.9 %fusion.85 = (f32[8,128]{1,0:T(8,128)S(1)}, f32[8,128]{1,0:T(8,128)S(1)}, f32[8,128]{1,0:T(8,128)S(1)}, f32[8,128]{1,0:T(8,128)S(1)}) fusion(f32[]{:T(128)} %bitcast.154, f32[]{:T(128)} %bitcast.155, f32[]{:T(128)} %bitcast.156, f32[]{:T(128)} %bitcast.157, f32[]{:T(128)} %bitcast.158, f32[]{:T(128)} %bitcast.159, f32[8,8,128]{2,1,0:T(8,128)S(1)} %copy.83, ...), kind=kOutput, calls=%fused_computation.16.clone.1 | output fusion | flops 339968 | bytes 82008 | tf_op jit(solution)/shard_map/while/body/eval_jaxpr/jit(cumsum)/reduce_window_sum | solution.py:112
  51.3 1.3 %gather_fusion = f32[8,8,128]{1,0,2:T(8,128)S(1)} fusion(f32[8,8,256]{1,0,2:T(8,128)S(1)} %bitcast.166, s32[8]{0:T(128)S(1)} %get-tuple-element.294), kind=kCustom, calls=%fused_computation.1.clone.1 | custom fusion | bytes 65632 | tf_op jit(solution)/shard_map/while/body/eval_jaxpr/vmap()/gather | solution.py:102
  52.8 1.3 %gather_fusion.1 = f32[8,8,128]{1,0,2:T(8,128)S(1)} fusion(f32[8,8,256]{1,0,2:T(8,128)S(1)} %bitcast.167, s32[8]{0:T(128)S(1)} %get-tuple-element.296), kind=kCustom, calls=%fused_computation.clone.1 | custom fusion | bytes 65632 | tf_op jit(solution)/shard_map/while/body/eval_jaxpr/vmap()/gather | solution.py:101
  54.3 0.7 fusion.84
  55.7 3.9 %fusion.85 = (f32[8,128]{1,0:T(8,128)S(1)}, f32[8,128]{1,0:T(8,128)S(1)}, f32[8,128]{1,0:T(8,128)S(1)}, f32[8,128]{1,0:T(8,128)S(1)}) fusion(f32[]{:T(128)} %bitcast.154, f32[]{:T(128)} %bitcast.155, f32[]{:T(128)} %bitcast.156, f32[]{:T(128)} %bitcast.157, f32[]{:T(128)} %bitcast.158, f32[]{:T(128)} %bitcast.159, f32[8,8,128]{2,1,0:T(8,128)S(1)} %copy.83, ...), kind=kOutput, calls=%fused_computation.16.clone.1 | output fusion | flops 339968 | bytes 82008 | tf_op jit(solution)/shard_map/while/body/eval_jaxpr/jit(cumsum)/reduce_window_sum | solution.py:112
  61.6 1.3 %gather_fusion = f32[8,8,128]{1,0,2:T(8,128)S(1)} fusion(f32[8,8,256]{1,0,2:T(8,128)S(1)} %bitcast.166, s32[8]{0:T(128)S(1)} %get-tuple-element.294), kind=kCustom, calls=%fused_computation.1.clone.1 | custom fusion | bytes 65632 | tf_op jit(solution)/shard_map/while/body/eval_jaxpr/vmap()/gather | solution.py:102
  63.1 1.3 %gather_fusion.1 = f32[8,8,128]{1,0,2:T(8,128)S(1)} fusion(f32[8,8,256]{1,0,2:T(8,128)S(1)} %bitcast.167, s32[8]{0:T(128)S(1)} %get-tuple-element.296), kind=kCustom, calls=%fused_computation.clone.1 | custom fusion | bytes 65632 | tf_op jit(solution)/shard_map/while/body/eval_jaxpr/vmap()/gather | solution.py:101
  64.6 0.7 fusion.84
  66.0 3.9 %fusion.85 = (f32[8,128]{1,0:T(8,128)S(1)}, f32[8,128]{1,0:T(8,128)S(1)}, f32[8,128]{1,0:T(8,128)S(1)}, f32[8,128]{1,0:T(8,128)S(1)}) fusion(f32[]{:T(128)} %bitcast.154, f32[]{:T(128)} %bitcast.155, f32[]{:T(128)} %bitcast.156, f32[]{:T(128)} %bitcast.157, f32[]{:T(128)} %bitcast.158, f32[]{:T(128)} %bitcast.159, f32[8,8,128]{2,1,0:T(8,128)S(1)} %copy.83, ...), kind=kOutput, calls=%fused_computation.16.clone.1 | output fusion | flops 339968 | bytes 82008 | tf_op jit(solution)/shard_map/while/body/eval_jaxpr/jit(cumsum)/reduce_window_sum | solution.py:112
  71.9 1.3 %gather_fusion = f32[8,8,128]{1,0,2:T(8,128)S(1)} fusion(f32[8,8,256]{1,0,2:T(8,128)S(1)} %bitcast.166, s32[8]{0:T(128)S(1)} %get-tuple-element.294), kind=kCustom, calls=%fused_computation.1.clone.1 | custom fusion | bytes 65632 | tf_op jit(solution)/shard_map/while/body/eval_jaxpr/vmap()/gather | solution.py:102
  73.4 1.3 %gather_fusion.1 = f32[8,8,128]{1,0,2:T(8,128)S(1)} fusion(f32[8,8,256]{1,0,2:T(8,128)S(1)} %bitcast.167, s32[8]{0:T(128)S(1)} %get-tuple-element.296), kind=kCustom, calls=%fused_computation.clone.1 | custom fusion | bytes 65632 | tf_op jit(solution)/shard_map/while/body/eval_jaxpr/vmap()/gather | solution.py:101
  74.9 0.7 fusion.84
  76.3 3.9 %fusion.85 = (f32[8,128]{1,0:T(8,128)S(1)}, f32[8,128]{1,0:T(8,128)S(1)}, f32[8,128]{1,0:T(8,128)S(1)}, f32[8,128]{1,0:T(8,128)S(1)}) fusion(f32[]{:T(128)} %bitcast.154, f32[]{:T(128)} %bitcast.155, f32[]{:T(128)} %bitcast.156, f32[]{:T(128)} %bitcast.157, f32[]{:T(128)} %bitcast.158, f32[]{:T(128)} %bitcast.159, f32[8,8,128]{2,1,0:T(8,128)S(1)} %copy.83, ...), kind=kOutput, calls=%fused_computation.16.clone.1 | output fusion | flops 339968 | bytes 82008 | tf_op jit(solution)/shard_map/while/body/eval_jaxpr/jit(cumsum)/reduce_window_sum | solution.py:112
  81.2 8.5 %all_to_all.5 = f32[4,1,4096]{2,1,0:T(1,128)S(1)} all-to-all(f32[4,1,4096]{2,1,0:T(1,128)S(1)} %reshape.256), channel_id=1, replica_groups=mesh['gx'=8,'gy'=4] {'gy'}, dimensions={0} | all-to-all | bytes 131072 | tf_op jit(solution)/shard_map/all_to_all | solution.py:163
  90.2 0.8 reduce.21
  (115 shorter events, 17.5 us)
Async XLA Ops:
  2.4 0.8 copy-start.2
  2.4 1.5 %copy-start.3 = (f32[8,8,128]{2,1,0:T(8,128)S(1)}, f32[8,8,128]{2,1,0:T(8,128)}, u32[]{:S(2)}) copy-start(f32[8,8,128]{2,1,0:T(8,128)} %param.13) | copy-start | bytes 98308
  3.9 0.8 copy-start.5
  12.3 7.6 %copy-start.4 = (s32[8,8,128]{2,1,0:T(8,128)S(1)}, s32[8,8,128]{2,1,0:T(8,128)}, u32[]{:S(2)}) copy-start(s32[8,8,128]{2,1,0:T(8,128)} %param.15) | copy-start | bytes 98308
  19.9 4.3 %collective-permute-start = (f32[5,2,8,128]{3,2,1,0:T(8,128)S(1)}, f32[5,2,8,128]{3,2,1,0:T(8,128)S(1)}, u32[]{:S(2)}, u32[]{:S(2)}) collective-permute-start(f32[5,2,8,128]{3,2,1,0:T(8,128)S(1)} %get-tuple-element.191), channel_id=1, source_target_pairs={{0,4},{4,8},{8,12},{12,16},{16,20},{20,24},{24,28},{1,5},{5,9},{9,... | collective-permute-start | bytes 122888 | tf_op jit(solution)/shard_map/ppermute | solution.py:18
  22.3 5.3 %collective-permute-start.1 = (f32[5,2,8,128]{3,2,1,0:T(8,128)S(1)}, f32[5,2,8,128]{3,2,1,0:T(8,128)S(1)}, u32[]{:S(2)}, u32[]{:S(2)}) collective-permute-start(f32[5,2,8,128]{3,2,1,0:T(8,128)S(1)} %get-tuple-element.192), channel_id=1, source_target_pairs={{4,0},{8,4},{12,8},{16,12},{20,16},{24,20},{28,24},{5,1},{9,5},{13... | collective-permute-start | bytes 122888 | tf_op jit(solution)/shard_map/ppermute | solution.py:19
  27.7 5.3 %collective-permute-start.2 = (f32[5,12,2,128]{3,2,1,0:T(2,128)S(1)}, f32[5,12,2,128]{3,2,1,0:T(2,128)S(1)}, u32[]{:S(2)}, u32[]{:S(2)}) collective-permute-start(f32[5,12,2,128]{3,2,1,0:T(2,128)S(1)} %get-tuple-element.189), channel_id=1, source_target_pairs={{0,1},{1,2},{2,3},{4,5},{5,6},{6,7},{8,9},{9,10},{10,11},{12,13},{... | collective-permute-start | bytes 184328 | tf_op jit(solution)/shard_map/ppermute | solution.py:18
  31.1 6.1 %collective-permute-start.3 = (f32[5,12,2,128]{3,2,1,0:T(2,128)S(1)}, f32[5,12,2,128]{3,2,1,0:T(2,128)S(1)}, u32[]{:S(2)}, u32[]{:S(2)}) collective-permute-start(f32[5,12,2,128]{3,2,1,0:T(2,128)S(1)} %get-tuple-element.190), channel_id=1, source_target_pairs={{1,0},{2,1},{3,2},{5,4},{6,5},{7,6},{9,8},{10,9},{11,10},{13,12},{... | collective-permute-start | bytes 184328 | tf_op jit(solution)/shard_map/ppermute | solution.py:19
  39.1 0.7 copy-start
  39.1 0.7 copy-start.1
  39.1 0.7 copy-start.7
  91.3 0.7 copy-start.6
